TPU v7x, 128 devices: a whole 4x4x4 slice. The times are simulated.
128 devices in a mesh: ctx: 32 (over z, y, core), head: 4 (over x).
Axes of the slice: x: 4, y: 4, z: 4, core: 2. Of those that a mesh axis runs over, the one named last changes fastest.
Arguments:
- queries: bfloat16 [49152, 2048], P('ctx', 'head'), may hold values from -20 to 20
- keys: bfloat16 [49152, 2048], P('ctx', 'head'), may hold values from -20 to 20
- values: bfloat16 [49152, 2048], P('ctx', 'head'), may hold values from -6 to 6
- offsets: int32 [3, 16], replicated, may hold values from 0 to 7, as said below
- out_weight: bfloat16 [2048, 2048], replicated, may hold values from -1.1953125 to 1.1953125
Outputs:
- mixed: bfloat16 [49152, 2048], P(('ctx', 'head'))
Inputs may be any that keep to these rules, and one draw needn't show every extreme that they name: `offsets`: each offset of row k - 1 lies in 0 to 2^k - 1; in the last row every value of that range occurs.
All inputs are finite; a program needn't handle non-finite values.
Results may differ from a plain program's by a relative error of at most 0.0053.
Values may be sent and summed in bfloat16 or wider, within the bound.
A program may use at most 192 MiB of HBM per device.

v0:
```python
import math
import jax
import jax.numpy as jnp
from jax import lax
from jax.sharding import PartitionSpec as P

DH = 128
LEVELS = 4
NEG_FILL = -1e30


def swapped(value, axis, bit):
    mask = 2**bit
    pairs = [(source, source ^ mask) for source in range(lax.axis_size(axis))]
    return lax.ppermute(value, axis, pairs)


def pick_rows(source, shifts, dilation):
    hits = jnp.arange(dilation)[:, None] == shifts[None, :]
    shaped = source.reshape(source.shape[0] // dilation, dilation, source.shape[1], source.shape[2])
    return jnp.sum(jnp.where(hits[None, :, :, None], shaped, jnp.zeros((), source.dtype)), axis=1)


def block_attend(query_rows, key_rows, value_rows, query_pos):
    number = query_rows.shape[0]
    heads_here = query_rows.shape[1]
    width_head = query_rows.shape[2]
    height = 512 if number % 512 == 0 else number
    blocks = number // height
    key_pos = jnp.arange(key_rows.shape[0])
    factor = 1.0 / math.sqrt(width_head)

    def one_block(items):
        rows_now, pos_now = items
        scores = (
            jnp.einsum("qhd,khd->hqk", rows_now, key_rows, preferred_element_type=jnp.float32)
            * factor
        )
        scores = jnp.where(pos_now[None, :, None] >= key_pos[None, None, :], scores, NEG_FILL)
        row_max = jnp.max(scores, axis=2)
        weights = jnp.exp(scores - row_max[:, :, None])
        row_sum = jnp.sum(weights, axis=2)
        weighted = jnp.einsum(
            "hqk,khd->qhd",
            weights.astype(jnp.bfloat16),
            value_rows,
            preferred_element_type=jnp.float32,
        )
        return (row_max.T, row_sum.T, weighted)

    shaped_rows = query_rows.reshape(blocks, height, heads_here, width_head)
    maxima, sums_all, outputs = lax.map(one_block, (shaped_rows, query_pos.reshape(blocks, height)))
    return (
        maxima.reshape(number, heads_here),
        sums_all.reshape(number, heads_here),
        outputs.reshape(number, heads_here, width_head),
    )


def spread_rows(parts, shifts, dilation):
    row_max, row_sum, weighted = parts
    hits = jnp.arange(dilation)[:, None] == shifts[None, :]
    number = row_max.shape[0] * dilation
    heads_here = row_max.shape[1]
    full_max = jnp.where(hits[None], row_max[:, None, :], NEG_FILL).reshape(number, heads_here)
    full_sum = jnp.where(hits[None], row_sum[:, None, :], 0.0).reshape(number, heads_here)
    full_out = jnp.where(hits[None, :, :, None], weighted[:, None], 0.0).reshape(
        number, heads_here, weighted.shape[2]
    )
    return (full_max, full_sum, full_out)


def merge_levels(running, fresh):
    new_max = jnp.maximum(running[0], fresh[0])
    old_scale = jnp.exp(running[0] - new_max)
    new_scale = jnp.exp(fresh[0] - new_max)
    new_sum = running[1] * old_scale + fresh[1] * new_scale
    new_out = running[2] * old_scale[:, :, None] + fresh[2] * new_scale[:, :, None]
    return (new_max, new_sum, new_out)


def join_pair(mine, partner, ctx_index, bit_index):
    upper = ctx_index // 2**bit_index % 2 == 1
    joined = []
    for mine_part, other_part in zip(mine, partner):
        joined.append(
            jnp.where(
                upper,
                jnp.concatenate([other_part, mine_part], 0),
                jnp.concatenate([mine_part, other_part], 0),
            )
        )
    return tuple(joined)


def body(queries, keys, values, offsets, out_weight):
    rows_here = queries.shape[0]
    head_count = lax.axis_size("head")
    heads_here = offsets.shape[1] // head_count
    query_heads = queries.reshape(rows_here, heads_here, DH)
    key_heads = keys.reshape(rows_here, heads_here, DH)
    value_heads = values.reshape(rows_here, heads_here, DH)
    ctx_index = lax.axis_index("ctx")
    shifts_here = lax.dynamic_slice_in_dim(
        offsets, lax.axis_index("head") * heads_here, heads_here, 1
    )
    running = block_attend(query_heads, key_heads, value_heads, jnp.arange(rows_here))
    group = (key_heads, value_heads)
    sources = []
    for bit_index in range(LEVELS - 1):
        partner = swapped((group[0], group[1]), "ctx", bit_index)
        group = join_pair(group, partner, ctx_index, bit_index)
        dilation = 2 ** (bit_index + 1)
        sources.append(
            (
                pick_rows(group[0], shifts_here[bit_index], dilation),
                pick_rows(group[1], shifts_here[bit_index], dilation),
            )
        )
    for level_index in range(1, LEVELS):
        dilation = 2**level_index
        shifts_now = shifts_here[level_index - 1]
        query_rows = pick_rows(query_heads, shifts_now, dilation)
        span = rows_here // dilation
        query_pos = ctx_index % dilation * span + jnp.arange(span)
        parts = block_attend(
            query_rows, sources[level_index - 1][0], sources[level_index - 1][1], query_pos
        )
        running = merge_levels(running, spread_rows(parts, shifts_now, dilation))
    attended = (
        (running[2] / running[1][:, :, None])
        .astype(jnp.bfloat16)
        .reshape(rows_here, heads_here * DH)
    )
    regrouped = lax.all_to_all(attended, "head", split_axis=0, concat_axis=1, tiled=True)
    mixed = jnp.dot(regrouped, out_weight, preferred_element_type=jnp.float32)
    return mixed.astype(jnp.bfloat16)


def solution(mesh):
    placed = (P("ctx", "head"), P("ctx", "head"), P("ctx", "head"), P(), P())
    return jax.shard_map(
        body, mesh=mesh, in_specs=placed, out_specs=P(("ctx", "head"), None), check_vma=False
    )
```

profile of v0, /device:TPU:0, one launch (start us, length us, event | category | flops | bytes accessed | tf_op | source)
XLA Modules:
  0.0 672.1 jit_solution(2948327554374246019)
XLA Ops:
  10.3 3.5 reshape_reshape.13
  13.9 3.5 reshape_reshape.12
  17.3 3.6 reshape_reshape.14
  22.7 45.2 %while.3 = (s32[]{:T(128)}, f32[3,512,4]{1,2,0:T(4,128)S(1)}, f32[3,512,4]{1,2,0:T(4,128)}, f32[3,512,4,128]{3,2,1,0:T(4,128)}, s32[3,512]{1,0:T(4,128)S(1)}, /*...) while((s32[]{:T(128)}, f32[3,512,4]{1,2,0:T(4,128)S(1)}, ...), condition=%wide.region_3.4_spmd.clone, body=%wide.region_0.3_spmd.clone.sunk | while | flops 1645998080 | bytes 48830580 | solution.py:52
  24.5 2.8 fusion.84
  27.3 3.6 fusion.85
  30.9 4.5 fusion.86
  39.5 2.8 fusion.84
  42.3 3.6 fusion.85
  46.0 4.5 fusion.86
  54.5 2.8 fusion.84
  57.4 3.6 fusion.85
  61.0 4.5 fusion.86
  68.0 4.2 select_reduce_fusion.3
  72.7 3.8 select_reduce_fusion.2
  81.5 3.9 maximum_select_fusion.5
  91.7 5.8 broadcast_in_dim.426
  97.5 3.2 broadcast_in_dim.427
  100.7 6.7 broadcast_in_dim.441
  107.3 3.2 broadcast_in_dim.442
  110.5 5.8 broadcast_in_dim.455
  116.3 3.1 broadcast_in_dim.456
  119.4 5.0 reshape.576
  127.5 5.1 maximum_select_fusion.4
  132.6 4.6 copy.77
  137.6 42.4 %fusion.32 = (bf16[1536,4,128]{2,0,1:T(8,128)(2,1)S(1)}, bf16[1536,4,128]{2,0,1:T(8,128)(2,1)S(1)}) fusion(bf16[1536,2,4,128]{3,1,0,2:T(2,128)(2,1)} %bitcast.100, pred[2,4]{0,1:T(4,128)(4,1)S(1)} %copy-done.28, bf16[1536,2,4,128]{3,1,0,2:T(2,128)(2,1)} %bitcast.101), kind=kLoop, calls=%fused_computation.52 | loop fusion | flops 4718592 | bytes 9437192 | tf_op jit(solution)/shard_map/reduce_sum | solution.py:21
  180.1 8.7 %fusion.14 = (f32[4,768]{1,0:T(4,128)S(1)}, f32[4,768,1536]{2,1,0:T(8,128)}) fusion(pred[768,1536]{1,0:T(8,128)(4,1)S(1)} %copy-done.5, bf16[1536,4,128]{2,0,1:T(8,128)(2,1)S(1)} %get-tuple-element.181, bf16[768,4,128]{2,1,0:T(4,128)(2,1)S(1)} %copy-done.10), kind=kOutput, calls=%fused_computation.21 | convolution fusion | flops 1222112256 | bytes 22425600 | tf_op jit(solution)/shard_map/while/body/eval_jaxpr/qhd,khd->hqk/dot_general | solution.py:36
  188.7 7.1 %maximum_select_fusion.3 = bf16[6144,4,128]{0,2,1:T(8,128)(2,1)} fusion(bf16[3072,4,128]{0,2,1:T(8,128)(2,1)S(1)} %maximum_select_fusion.5, bf16[3072,4,128]{0,2,1:T(8,128)(2,1)} %collective-permute-done.3, pred[]{:T(512)S(6)} %eq.62), kind=kLoop, calls=%fused_computation.38 | loop fusion | flops 28311552 | bytes 12582913 | tf_op jit(solution)/shard_map/jit(_where)/select_n | solution.py:87
  195.8 3.3 collective-permute-start.5
  199.1 10.6 %fusion.40 = f32[768,4,128]{0,2,1:T(8,128)} fusion(bf16[1536,4,128]{2,0,1:T(8,128)(2,1)S(1)} %get-tuple-element.180, f32[4,768,1536]{2,1,0:T(8,128)} %get-tuple-element.221, f32[4,768]{1,0:T(4,128)S(1)} %get-tuple-element.220, pred[768,1536]{1,0:T(8,128)(4,1)S(1)} %copy-done.5), kind=kOutput, calls=%fused_computation.67 | convolution fusion | flops 1226833920 | bytes 23212032 | tf_op jit(solution)/shard_map/while/body/eval_jaxpr/hqk,khd->qhd/dot_general | solution.py:43
  213.4 10.6 %collective-permute-done.2 = bf16[3072,4,128]{0,2,1:T(8,128)(2,1)} collective-permute-done((bf16[3072,4,128]{0,2,1:T(8,128)(2,1)}, bf16[3072,4,128]{0,2,1:T(8,128)(2,1)}, u32[]{:S(2)}, u32[]{:S(2)}) %collective-permute-start.2) | collective-permute-done | bytes 3145760 | tf_op jit(solution)/shard_map/ppermute | solution.py:15
  224.0 7.1 %maximum_select_fusion.2 = bf16[6144,4,128]{0,2,1:T(8,128)(2,1)} fusion(bf16[3072,4,128]{0,2,1:T(8,128)(2,1)S(1)} %copy-done.3, bf16[3072,4,128]{0,2,1:T(8,128)(2,1)} %collective-permute-done.2, pred[]{:T(512)S(6)} %eq.62), kind=kLoop, calls=%fused_computation.37 | loop fusion | flops 28311552 | bytes 12582913 | tf_op jit(solution)/shard_map/jit(_where)/select_n | solution.py:87
  231.1 3.3 collective-permute-start.4
  234.4 9.2 %fusion.15 = f32[4,768]{1,0:T(4,128)S(1)} fusion(f32[4,768,1536]{2,1,0:T(8,128)} %get-tuple-element.221, f32[4,768]{1,0:T(4,128)S(1)} %get-tuple-element.220, pred[768,1536]{1,0:T(8,128)(4,1)S(1)} %copy-done.6), kind=kLoop, calls=%fused_computation.22 | loop fusion | flops 18871296 | bytes 20078592 | tf_op jit(solution)/shard_map/while/body/eval_jaxpr/reduce_sum | solution.py:42
  250.7 8.7 %copy.92 = bf16[6144,4,128]{2,0,1:T(8,128)(2,1)} copy(bf16[6144,4,128]{0,2,1:T(8,128)(2,1)} %maximum_select_fusion.3) | data formatting | bytes 12582912 | tf_op jit(solution)/shard_map/jit(_where)/select_n | solution.py:87
  259.4 8.6 %copy.88 = bf16[6144,4,128]{2,0,1:T(8,128)(2,1)} copy(bf16[6144,4,128]{0,2,1:T(8,128)(2,1)} %maximum_select_fusion.2) | data formatting | bytes 12582912 | tf_op jit(solution)/shard_map/jit(_where)/select_n | solution.py:87
  268.0 42.8 %select_reduce_fusion = (bf16[1536,4,128]{2,0,1:T(8,128)(2,1)S(1)}, bf16[1536,4,128]{2,0,1:T(8,128)(2,1)S(1)}) fusion(bf16[1536,4,4,128]{3,1,0,2:T(4,128)(2,1)} %bitcast.97, pred[4,4]{0,1:T(4,128)(4,1)S(1)} %copy-done.26, bf16[1536,4,4,128]{3,1,0,2:T(4,128)(2,1)} %bitcast.98), kind=kLoop, calls=%fused_computation.39 | loop fusion | flops 11010048 | bytes 15728656 | tf_op jit(solution)/shard_map/reduce_sum | solution.py:21
  313.0 3.6 copy-done.2
  316.6 3.9 fusion.43
  324.2 6.4 fusion.23
  333.5 2.8 broadcast_in_dim.444
  336.3 25.0 %collective-permute-done.5 = bf16[6144,4,128]{0,2,1:T(8,128)(2,1)} collective-permute-done((bf16[6144,4,128]{0,2,1:T(8,128)(2,1)}, bf16[6144,4,128]{0,2,1:T(8,128)(2,1)}, u32[]{:S(2)}, u32[]{:S(2)}) %collective-permute-start.5) | collective-permute-done | bytes 6291488 | tf_op jit(solution)/shard_map/ppermute | solution.py:15
  361.4 15.6 %maximum_select_fusion.1 = bf16[12288,4,128]{0,2,1:T(8,128)(2,1)} fusion(bf16[6144,4,128]{0,2,1:T(8,128)(2,1)} %maximum_select_fusion.3, bf16[6144,4,128]{0,2,1:T(8,128)(2,1)} %collective-permute-done.5, pred[]{:T(512)S(6)} %eq.66), kind=kLoop, calls=%fused_computation.25 | loop fusion | flops 56623104 | bytes 25165824 | tf_op jit(solution)/shard_map/jit(_where)/select_n | solution.py:87
  377.0 16.6 %copy.100 = bf16[12288,4,128]{2,0,1:T(8,128)(2,1)} copy(bf16[12288,4,128]{0,2,1:T(8,128)(2,1)} %maximum_select_fusion.1) | data formatting | bytes 25165824 | tf_op jit(solution)/shard_map/jit(_where)/select_n | solution.py:87
  393.6 101.6 %collective-permute-done.4 = bf16[6144,4,128]{0,2,1:T(8,128)(2,1)} collective-permute-done((bf16[6144,4,128]{0,2,1:T(8,128)(2,1)}, bf16[6144,4,128]{0,2,1:T(8,128)(2,1)}, u32[]{:S(2)}, u32[]{:S(2)}) %collective-permute-start.4) | collective-permute-done | bytes 6291488 | tf_op jit(solution)/shard_map/ppermute | solution.py:15
  495.3 15.5 %maximum_select_fusion = bf16[12288,4,128]{0,2,1:T(8,128)(2,1)} fusion(bf16[6144,4,128]{0,2,1:T(8,128)(2,1)} %maximum_select_fusion.2, bf16[6144,4,128]{0,2,1:T(8,128)(2,1)} %collective-permute-done.4, pred[]{:T(512)S(6)} %eq.66), kind=kLoop, calls=%fused_computation.24 | loop fusion | flops 56623104 | bytes 25165824 | tf_op jit(solution)/shard_map/jit(_where)/select_n | solution.py:87
  510.8 16.6 %copy.96 = bf16[12288,4,128]{2,0,1:T(8,128)(2,1)} copy(bf16[12288,4,128]{0,2,1:T(8,128)(2,1)} %maximum_select_fusion) | data formatting | bytes 25165824 | tf_op jit(solution)/shard_map/jit(_where)/select_n | solution.py:87
  527.3 38.2 %fusion.17 = (bf16[1536,4,128]{2,0,1:T(8,128)(2,1)S(1)}, bf16[1536,4,128]{2,0,1:T(8,128)(2,1)S(1)}) fusion(bf16[12288,4,128]{2,0,1:T(8,128)(2,1)} %copy.100, pred[8,4]{0,1:T(4,128)(4,1)S(1)} %iota_compare_fusion.4, bf16[12288,4,128]{2,0,1:T(8,128)(2,1)} %copy.96), kind=kLoop, calls=%fused_computation.27 | loop fusion | flops 23592960 | bytes 28311584 | tf_op jit(solution)/shard_map/reduce_sum | solution.py:21
  579.2 3.3 mul.163
  582.6 2.8 mul.164
  585.4 3.3 mul.160
  588.7 2.9 mul.161
  591.6 3.3 mul.155
  594.9 2.9 mul.156
  597.8 3.3 mul.152
  603.9 3.3 mul.147
  607.2 2.9 mul.148
  610.1 3.3 mul.144
  613.4 2.9 mul.145
  616.3 4.3 div.34
  620.6 5.4 div.35
  627.8 10.9 %divide_convert_fusion = bf16[4,384,512]{2,1,0:T(8,128)(2,1)S(1)} fusion(f32[4,384,512]{2,1,0:T(8,128)} %div.35, f32[4,384,512]{2,1,0:T(8,128)} %mul.164, pred[4,384,512]{2,1,0:T(8,128)(4,1)} %broadcast_in_dim.456, f32[4,384,512]{2,1,0:T(8,128)S(1)} %bitcast.99, f32[4,384,512]{2,1,0:T(8,128)} %mul.161, f32[4,384,512]{2,1,0:T(8,128)} %mul.156, ...), kind=kLoop, calls=%fused_computation.55 | loop fusion | flops 11010048 | bytes 38535168 | tf_op jit(solution)/shard_map/convert_element_type | solution.py:132
  638.8 24.1 %all_to_all.16 = bf16[4,384,512]{2,1,0:T(8,128)(2,1)S(1)} all-to-all(bf16[4,384,512]{2,1,0:T(8,128)(2,1)S(1)} %divide_convert_fusion), channel_id=1, replica_groups=mesh['ctx'=32,'head'=4] {'head'}, dimensions={0} | all-to-all | bytes 3145728 | tf_op jit(solution)/shard_map/all_to_all | solution.py:135
  663.8 8.1 %convolution_convert_fusion = bf16[384,2048]{1,0:T(8,128)(2,1)} fusion(bf16[384,2048]{0,1:T(8,128)(2,1)S(1)} %bitcast.105, bf16[2048,2048]{1,0:T(8,128)(2,1)} %param.11), kind=kOutput, calls=%fused_computation.56 | convolution fusion | flops 3222011904 | bytes 11534336 | tf_op jit(solution)/shard_map/dot_general | solution.py:136
  (148 shorter events, 77.8 us)
Async XLA Ops:
  0.0 20.9 %copy-start = (s32[3,16]{1,0:T(4,128)S(1)}, s32[3,16]{1,0:T(4,128)}, u32[]{:S(2)}) copy-start(s32[3,16]{1,0:T(4,128)} %param.10) | copy-start | bytes 580
  2.6 78.9 %collective-permute-start.1 = (bf16[1536,4,128]{0,2,1:T(8,128)(2,1)}, bf16[1536,4,128]{0,2,1:T(8,128)(2,1)}, u32[]{:S(2)}, u32[]{:S(2)}) collective-permute-start(bf16[1536,4,128]{0,2,1:T(8,128)(2,1)} %bitcast.1), channel_id=1, source_target_pairs={{0,4},{4,0},{8,12},{12,8},{16,20},{20,16},{24,28},{28,24},{32,36},... | collective-permute-start | bytes 4718600 | tf_op jit(solution)/shard_map/ppermute | solution.py:15
  5.2 122.3 %collective-permute-start = (bf16[1536,4,128]{0,2,1:T(8,128)(2,1)}, bf16[1536,4,128]{0,2,1:T(8,128)(2,1)}, u32[]{:S(2)}, u32[]{:S(2)}) collective-permute-start(bf16[1536,4,128]{0,2,1:T(8,128)(2,1)} %bitcast), channel_id=1, source_target_pairs={{0,4},{4,0},{8,12},{12,8},{16,20},{20,16},{24,28},{28,24},{32,36},... | collective-permute-start | bytes 4718600 | tf_op jit(solution)/shard_map/ppermute | solution.py:15
  21.1 1.6 copy-start.27
  21.2 65.9 %copy-start.25 = (pred[4,4]{0,1:T(4,128)(4,1)}, pred[4,4]{0,1:T(4,128)(4,1)S(1)}, u32[]{:S(2)}) copy-start(pred[4,4]{0,1:T(4,128)(4,1)S(1)} %iota_compare_fusion.5) | copy-start | bytes 52
  21.7 1.0 copy-start.19
  68.0 17.5 %copy-start.23 = (f32[3,512,4]{1,2,0:T(4,128)}, f32[3,512,4]{1,2,0:T(4,128)S(1)}, u32[]{:S(2)}) copy-start(f32[3,512,4]{1,2,0:T(4,128)S(1)} %get-tuple-element.116) | copy-start | bytes 73732
  68.0 9.8 %copy-start.4 = (bf16[1536,512]{1,0:T(8,128)(2,1)S(1)}, bf16[1536,512]{1,0:T(8,128)(2,1)}, u32[]{:S(2)}) copy-start(bf16[1536,512]{1,0:T(8,128)(2,1)} %param.7) | copy-start | bytes 4718596
  77.8 10.9 %copy-start.28 = (pred[2,4]{0,1:T(4,128)(4,1)S(1)}, pred[2,4]{0,1:T(4,128)(4,1)}, u32[]{:S(2)}) copy-start(pred[2,4]{0,1:T(4,128)(4,1)} %copy-done.27) | copy-start | bytes 28
  85.4 103.3 %collective-permute-start.3 = (bf16[3072,4,128]{0,2,1:T(8,128)(2,1)S(1)}, bf16[3072,4,128]{0,2,1:T(8,128)(2,1)}, u32[]{:S(2)}, u32[]{:S(2)}) collective-permute-start(bf16[3072,4,128]{0,2,1:T(8,128)(2,1)S(1)} %maximum_select_fusion.5), channel_id=1, source_target_pairs={{0,8},{4,12},{8,0},{12,4},{16,24},{20,28},{24,16},{28,20},{32,40},... | collective-permute-start | bytes 9437192 | tf_op jit(solution)/shard_map/ppermute | solution.py:15
  90.6 19.9 %copy-start.14 = (pred[1536,4]{1,0:T(8,128)(4,1)S(1)}, pred[1536,4]{1,0:T(8,128)(4,1)}, u32[]{:S(2)}) copy-start(pred[1536,4]{1,0:T(8,128)(4,1)} %copy.99) | copy-start | bytes 18436
  110.5 14.0 %copy-start.29 = (s32[192]{0:T(256)S(1)}, s32[192]{0:T(256)}, u32[]{:S(2)}) copy-start(s32[192]{0:T(256)} %iota_add_fusion.2) | copy-start | bytes 2308
  137.2 86.8 %collective-permute-start.2 = (bf16[3072,4,128]{0,2,1:T(8,128)(2,1)}, bf16[3072,4,128]{0,2,1:T(8,128)(2,1)}, u32[]{:S(2)}, u32[]{:S(2)}) collective-permute-start(bf16[3072,4,128]{0,2,1:T(8,128)(2,1)} %maximum_select_fusion.4), channel_id=1, source_target_pairs={{0,8},{4,12},{8,0},{12,4},{16,24},{20,28},{24,16},{28,20},{32,40},... | collective-permute-start | bytes 9437192 | tf_op jit(solution)/shard_map/ppermute | solution.py:15
  137.6 42.4 %copy-start.5 = (pred[768,1536]{1,0:T(8,128)(4,1)S(1)}, pred[768,1536]{1,0:T(8,128)(4,1)}, u32[]{:S(2)}) copy-start(pred[768,1536]{1,0:T(8,128)(4,1)} %iota_compare_fusion.1) | copy-start | bytes 3538948
  137.6 42.5 %copy-start.10 = (bf16[768,4,128]{2,1,0:T(4,128)(2,1)S(1)}, bf16[768,4,128]{2,1,0:T(4,128)(2,1)}, u32[]{:S(2)}) copy-start(bf16[768,4,128]{2,1,0:T(4,128)(2,1)} %select_reduce_fusion.3) | copy-start | bytes 2359300
  195.8 165.6 %collective-permute-start.5 = (bf16[6144,4,128]{0,2,1:T(8,128)(2,1)}, bf16[6144,4,128]{0,2,1:T(8,128)(2,1)}, u32[]{:S(2)}, u32[]{:S(2)}) collective-permute-start(bf16[6144,4,128]{0,2,1:T(8,128)(2,1)} %maximum_select_fusion.3), channel_id=1, source_target_pairs={{0,16},{4,20},{8,24},{12,28},{16,0},{20,4},{24,8},{28,12},{32,48},... | collective-permute-start | bytes 18874376 | tf_op jit(solution)/shard_map/ppermute | solution.py:15
  209.7 14.2 %copy-start.3 = (bf16[3072,4,128]{0,2,1:T(8,128)(2,1)S(1)}, bf16[3072,4,128]{0,2,1:T(8,128)(2,1)}, u32[]{:S(2)}) copy-start(bf16[3072,4,128]{0,2,1:T(8,128)(2,1)} %maximum_select_fusion.4) | copy-start | bytes 9437188
  213.4 21.0 %copy-start.6 = (pred[768,1536]{1,0:T(8,128)(4,1)S(1)}, pred[768,1536]{1,0:T(8,128)(4,1)}, u32[]{:S(2)}) copy-start(pred[768,1536]{1,0:T(8,128)(4,1)} %iota_compare_fusion.1) | copy-start | bytes 3538948
  231.1 13.9 %copy-start.12 = (f32[768,4]{1,0:T(8,128)S(1)}, f32[768,4]{1,0:T(8,128)}, u32[]{:S(2)}) copy-start(f32[768,4]{1,0:T(8,128)} %copy.79) | copy-start | bytes 36868
  231.1 264.2 %collective-permute-start.4 = (bf16[6144,4,128]{0,2,1:T(8,128)(2,1)}, bf16[6144,4,128]{0,2,1:T(8,128)(2,1)}, u32[]{:S(2)}, u32[]{:S(2)}) collective-permute-start(bf16[6144,4,128]{0,2,1:T(8,128)(2,1)} %maximum_select_fusion.2), channel_id=1, source_target_pairs={{0,16},{4,20},{8,24},{12,28},{16,0},{20,4},{24,8},{28,12},{32,48},... | collective-permute-start | bytes 18874376 | tf_op jit(solution)/shard_map/ppermute | solution.py:15
  259.4 8.6 %copy-start.26 = (pred[4,4]{0,1:T(4,128)(4,1)S(1)}, pred[4,4]{0,1:T(4,128)(4,1)}, u32[]{:S(2)}) copy-start(pred[4,4]{0,1:T(4,128)(4,1)} %copy-done.25) | copy-start | bytes 52
  268.0 42.8 %copy-start.9 = (pred[384,1536]{1,0:T(8,128)(4,1)S(1)}, pred[384,1536]{1,0:T(8,128)(4,1)}, u32[]{:S(2)}) copy-start(pred[384,1536]{1,0:T(8,128)(4,1)} %iota_compare_fusion.2) | copy-start | bytes 1769476
  268.0 42.8 %copy-start.11 = (bf16[384,4,128]{2,1,0:T(4,128)(2,1)S(1)}, bf16[384,4,128]{2,1,0:T(4,128)(2,1)}, u32[]{:S(2)}) copy-start(bf16[384,4,128]{2,1,0:T(4,128)(2,1)} %select_reduce_fusion.2) | copy-start | bytes 1179652
  313.0 3.6 copy-start.2
  527.3 38.2 %copy-start.13 = (bf16[192,4,128]{2,1,0:T(4,128)(2,1)S(1)}, bf16[192,4,128]{2,1,0:T(4,128)(2,1)}, u32[]{:S(2)}) copy-start(bf16[192,4,128]{2,1,0:T(4,128)(2,1)} %fusion.39) | copy-start | bytes 589828
  568.1 2.6 copy-start.15
  568.1 2.6 copy-start.16
  568.1 2.6 copy-start.17
  568.1 2.6 copy-start.18
  568.1 2.6 copy-start.20
  568.2 2.6 copy-start.21
  568.2 2.6 copy-start.22
  568.2 2.6 copy-start.24
  620.6 5.8 copy-start.7
  626.0 1.9 copy-start.8
  663.8 8.1 %copy-start.1 = (s32[3,16]{1,0:T(4,128)S(1)}, s32[3,16]{1,0:T(4,128)}, u32[]{:S(2)}) copy-start(s32[3,16]{1,0:T(4,128)} %param.10) | copy-start | bytes 580
where the time goes:
time: 683 us; the launch traced here: 672 us
  other arithmetic  232 us (34%)
  local copies, waits for them, and re-layouts  210 us (31%)
  waiting for transfers between devices  137 us (20%)
  matrix products  58.1 us (9%)
  blocking collectives  24.1 us (4%)
  starting transfers between devices  9.23 us (1%)
    ppermute x6, waiting for transfers between devices, swapped(): return lax.ppermute(value, axis, pairs)  137 us
    reduce_sum x6, other arithmetic, pick_rows(): jnp.sum(jnp.where(hits[None, :, :, None], shaped, jnp.zeros((), source.dt...  133 us
    select_n x6, local copies, waits for them, and re-layouts, join_pair(): jnp.where(upper, jnp.concatenate([other_part, mine_part], 0), jnp.concate...  57.9 us
    select_n x6, other arithmetic, join_pair(): jnp.where(upper, jnp.concatenate([other_part, mine_part], 0), jnp.concate...  54.3 us
    dot_general x6, matrix products, one_block(): jnp.einsum('hqk,khd->qhd', weights.astype(jnp.bfloat16), value_rows, pref...  29.6 us
    reduce_sum x6, other arithmetic, one_block(): row_sum = jnp.sum(weights, axis=2)  27.9 us
    broadcast_in_dim x6, local copies, waits for them, and re-layouts, pick_rows(): jnp.where(hits[None, :, :, None], shaped, jnp.zeros((), source.dtype))  27.7 us
    all_to_all x1, blocking collectives, body(): lax.all_to_all(attended, 'head', split_axis=0, concat_axis=1, tiled=True)  24.1 us
  transfers between devices with their start and end apart: 6, of which 3 were waited for; matrix products, arithmetic and copies ran while one was open for 51% of the time, Pallas kernels for 0%

commit v1 on v0

--- a/solution.py
+++ b/solution.py
@@ -7,6 +7,13 @@
 DH = 128
 LEVELS = 4
 NEG_FILL = -1e30
+
+
+def trade_parts(block, axis, split, join):
+    size = lax.axis_size(axis)
+    blocks = jnp.stack(jnp.split(block, size, axis=split), axis=0)
+    blocks = lax.all_to_all(blocks, axis, split_axis=0, concat_axis=0)
+    return jnp.concatenate(blocks, axis=join)
 
 
 def swapped(value, axis, bit):
@@ -132,7 +139,7 @@
         .astype(jnp.bfloat16)
         .reshape(rows_here, heads_here * DH)
     )
-    regrouped = lax.all_to_all(attended, "head", split_axis=0, concat_axis=1, tiled=True)
+    regrouped = trade_parts(attended, "head", 0, 1)
     mixed = jnp.dot(regrouped, out_weight, preferred_element_type=jnp.float32)
     return mixed.astype(jnp.bfloat16)
 

time: 683 us -> 624 us (0.914)
  local copies, waits for them, and re-layouts: 210 us -> 103 us
  waiting for transfers between devices: 137 us -> 183 us
    ppermute x6, waiting for transfers between devices: 137 us -> 183 us  [swapped(): return lax.ppermute(value, axis, pairs)]
    mul x12 -> x0, local copies, waits for them, and re-layouts: 37 us -> none  [the longest x6 18.6 us: merge_levels(): fresh[2] * new_scale[:, :, None]]
    broadcast_in_dim x6 -> x0, local copies, waits for them, and re-layouts: 27.7 us -> none  [pick_rows(): jnp.where(hits[None, :, :, None], shaped, jnp.zeros((), source.dtype))]
    div x2 -> x0, local copies, waits for them, and re-layouts: 9.62 us -> none  [body(): running[2] / running[1][:, :, None]]
    broadcast_in_dim x5 -> x2, local copies, waits for them, and re-layouts: 9.43 us -> 1.62 us  [spread_rows(): jnp.where(hits[None, :, :, None], weighted[:, None], 0.0)]
    exp x6 -> x0, local copies, waits for them, and re-layouts: 7.17 us -> none  [the longest x3 3.59 us: merge_levels(): old_scale = jnp.exp(running[0] - new_max)]
    unnamed x64 -> x46, local copies, waits for them, and re-layouts: 15 us -> 13.9 us
  transfers between devices with their start and end apart: 6 -> 6, of which waited for: 3 -> 4; matrix products, arithmetic and copies ran while one was open for 51% -> 48% of each run, Pallas kernels for 0% -> 0%
where the time goes in v1:
time: 624 us; the launch traced here: 615 us
  other arithmetic  232 us (37%)
  waiting for transfers between devices  183 us (29%)
  local copies, waits for them, and re-layouts  103 us (17%)
  matrix products  62.3 us (10%)
  blocking collectives  24.1 us (4%)
  starting transfers between devices  9.23 us (1%)
    ppermute x6, waiting for transfers between devices, swapped(): return lax.ppermute(value, axis, pairs)  183 us
    reduce_sum x6, other arithmetic, pick_rows(): jnp.sum(jnp.where(hits[None, :, :, None], shaped, jnp.zeros((), source.dt...  133 us
    select_n x6, local copies, waits for them, and re-layouts, join_pair(): jnp.where(upper, jnp.concatenate([other_part, mine_part], 0), jnp.concate...  58 us
    select_n x6, other arithmetic, join_pair(): jnp.where(upper, jnp.concatenate([other_part, mine_part], 0), jnp.concate...  54.1 us
    dot_general x6, matrix products, one_block(): jnp.einsum('hqk,khd->qhd', weights.astype(jnp.bfloat16), value_rows, pref...  33.8 us
    reduce_sum x6, other arithmetic, one_block(): row_sum = jnp.sum(weights, axis=2)  28.3 us
    all_to_all x1, blocking collectives, trade_parts(): blocks = lax.all_to_all(blocks, axis, split_axis=0, concat_axis=0)  24.1 us
    dot_general x6, matrix products, one_block(): jnp.einsum('qhd,khd->hqk', rows_now, key_rows, preferred_element_type=jnp...  20.5 us
  transfers between devices with their start and end apart: 6, of which 4 were waited for; matrix products, arithmetic and copies ran while one was open for 48% of the time, Pallas kernels for 0%

profile of v1, /device:TPU:0, one launch (start us, length us, event | category | flops | bytes accessed | tf_op | source)
XLA Modules:
  0.0 614.9 jit_solution(4922505340865720858)
XLA Ops:
  0.0 2.6 copy.51
  2.6 2.6 copy.50
  5.7 2.0 copy.53
  7.8 2.7 copy.54
  10.4 3.5 reshape_reshape.13
  13.9 3.5 reshape_reshape.12
  17.4 3.5 reshape_reshape.14
  21.8 44.8 %while.3 = (s32[]{:T(128)}, f32[3,512,4]{1,2,0:T(4,128)S(1)}, f32[3,512,4]{1,2,0:T(4,128)}, f32[3,512,4,128]{3,1,0,2:T(8,128)}, s32[3,512]{1,0:T(4,128)S(1)}, /*...) while((s32[]{:T(128)}, f32[3,512,4]{1,2,0:T(4,128)S(1)}, ...), condition=%wide.region_3.4_spmd.clone, body=%wide.region_0.3_spmd.clone.sunk | while | flops 1645998080 | bytes 46733428 | solution.py:59
  21.8 1.2 constant_dynamic-slice_fusion.6
  23.6 2.8 fusion.96
  26.4 3.6 fusion.97
  30.0 5.9 fusion.98
  36.6 1.2 constant_dynamic-slice_fusion.6
  38.3 2.8 fusion.96
  41.2 3.6 fusion.97
  44.8 6.0 fusion.98
  51.4 1.2 constant_dynamic-slice_fusion.6
  53.1 2.8 fusion.96
  56.0 3.6 fusion.97
  59.6 6.0 fusion.98
  66.7 4.2 select_reduce_fusion.3
  71.4 3.9 select_reduce_fusion.2
  75.3 1.2 iota_compare_fusion.2
  76.4 1.9 fusion.50
  78.3 1.7 iota_compare_fusion.1
  80.1 3.7 maximum_select_fusion.5
  83.8 1.8 collective-permute-start.3
  87.2 1.7 broadcast_in_dim.410
  89.7 2.8 copy.61
  92.6 5.0 maximum_select_fusion.4
  97.6 4.6 copy.57
  102.6 42.2 %fusion.34 = (bf16[1536,4,128]{2,0,1:T(8,128)(2,1)S(1)}, bf16[1536,4,128]{2,0,1:T(8,128)(2,1)S(1)}) fusion(bf16[1536,2,4,128]{3,1,0,2:T(2,128)(2,1)} %bitcast.135, pred[2,4]{0,1:T(4,128)(4,1)S(1)} %copy-done.20, bf16[1536,2,4,128]{3,1,0,2:T(2,128)(2,1)} %bitcast.133), kind=kLoop, calls=%fused_computation.51 | loop fusion | flops 4718592 | bytes 9437192 | tf_op jit(solution)/shard_map/reduce_sum | solution.py:28
  144.8 8.7 %fusion.17 = (f32[4,768]{1,0:T(4,128)S(1)}, f32[4,768,1536]{2,1,0:T(8,128)}) fusion(pred[768,1536]{1,0:T(8,128)(4,1)S(1)} %copy-done.5, bf16[1536,4,128]{2,0,1:T(8,128)(2,1)S(1)} %get-tuple-element.182, bf16[768,4,128]{2,1,0:T(4,128)(2,1)S(1)} %copy-done.9), kind=kOutput, calls=%fused_computation.21 | convolution fusion | flops 1222112256 | bytes 22425600 | tf_op jit(solution)/shard_map/while/body/eval_jaxpr/qhd,khd->hqk/dot_general | solution.py:43
  153.5 1.5 collective-permute-done.3
  155.0 7.1 %maximum_select_fusion.3 = bf16[6144,4,128]{0,2,1:T(8,128)(2,1)} fusion(bf16[3072,4,128]{0,2,1:T(8,128)(2,1)S(1)} %maximum_select_fusion.5, bf16[3072,4,128]{0,2,1:T(8,128)(2,1)} %collective-permute-done.3, pred[]{:T(512)S(6)} %eq.62), kind=kLoop, calls=%fused_computation.38 | loop fusion | flops 28311552 | bytes 12582913 | tf_op jit(solution)/shard_map/jit(_where)/select_n | solution.py:94
  162.0 3.3 collective-permute-start.5
  165.3 10.4 %fusion.51 = f32[768,4,128]{0,2,1:T(8,128)} fusion(bf16[1536,4,128]{2,0,1:T(8,128)(2,1)S(1)} %get-tuple-element.183, f32[4,768,1536]{2,1,0:T(8,128)} %get-tuple-element.223, f32[4,768]{1,0:T(4,128)S(1)} %get-tuple-element.222, pred[768,1536]{1,0:T(8,128)(4,1)S(1)} %copy-done.5), kind=kOutput, calls=%fused_computation.77 | convolution fusion | flops 1226833920 | bytes 23212032 | tf_op jit(solution)/shard_map/while/body/eval_jaxpr/hqk,khd->qhd/dot_general | solution.py:50
  175.8 3.2 copy.63
  180.0 42.4 %collective-permute-done.2 = bf16[3072,4,128]{0,2,1:T(8,128)(2,1)} collective-permute-done((bf16[3072,4,128]{0,2,1:T(8,128)(2,1)}, bf16[3072,4,128]{0,2,1:T(8,128)(2,1)}, u32[]{:S(2)}, u32[]{:S(2)}) %collective-permute-start.2) | collective-permute-done | bytes 3145760 | tf_op jit(solution)/shard_map/ppermute | solution.py:22
  222.4 7.1 %maximum_select_fusion.2 = bf16[6144,4,128]{0,2,1:T(8,128)(2,1)} fusion(bf16[3072,4,128]{0,2,1:T(8,128)(2,1)S(1)} %copy-done.3, bf16[3072,4,128]{0,2,1:T(8,128)(2,1)} %collective-permute-done.2, pred[]{:T(512)S(6)} %eq.62), kind=kLoop, calls=%fused_computation.37 | loop fusion | flops 28311552 | bytes 12582913 | tf_op jit(solution)/shard_map/jit(_where)/select_n | solution.py:94
  229.5 3.3 collective-permute-start.4
  232.8 9.6 %fusion.18 = f32[4,768]{1,0:T(4,128)S(1)} fusion(f32[4,768,1536]{2,1,0:T(8,128)} %get-tuple-element.223, f32[4,768]{1,0:T(4,128)S(1)} %get-tuple-element.222, pred[768,1536]{1,0:T(8,128)(4,1)S(1)} %copy-done.6), kind=kLoop, calls=%fused_computation.22 | loop fusion | flops 18871296 | bytes 20078592 | tf_op jit(solution)/shard_map/while/body/eval_jaxpr/reduce_sum | solution.py:49
  243.7 8.6 %copy.67 = bf16[6144,4,128]{2,0,1:T(8,128)(2,1)} copy(bf16[6144,4,128]{0,2,1:T(8,128)(2,1)} %maximum_select_fusion.3) | data formatting | bytes 12582912 | tf_op jit(solution)/shard_map/jit(_where)/select_n | solution.py:94
  252.3 8.7 %copy.65 = bf16[6144,4,128]{2,0,1:T(8,128)(2,1)} copy(bf16[6144,4,128]{0,2,1:T(8,128)(2,1)} %maximum_select_fusion.2) | data formatting | bytes 12582912 | tf_op jit(solution)/shard_map/jit(_where)/select_n | solution.py:94
  261.0 42.6 %select_reduce_fusion.1 = (bf16[1536,4,128]{2,0,1:T(8,128)(2,1)S(1)}, bf16[1536,4,128]{2,0,1:T(8,128)(2,1)S(1)}) fusion(bf16[1536,4,4,128]{3,1,0,2:T(4,128)(2,1)} %bitcast.132, pred[4,4]{0,1:T(4,128)(4,1)S(1)} %copy-done.18, bf16[1536,4,4,128]{3,1,0,2:T(4,128)(2,1)} %bitcast.131), kind=kLoop, calls=%fused_computation.40 | loop fusion | flops 11010048 | bytes 15728656 | tf_op jit(solution)/shard_map/reduce_sum | solution.py:28
  303.6 2.1 fusion.25
  305.8 3.6 copy-done.2
  309.4 3.9 fusion.54
  313.3 1.4 copy.69
  315.4 6.4 %fusion.26 = f32[4,384]{1,0:T(4,128)S(1)} fusion(f32[4,384,1536]{2,1,0:T(8,128)} %copy-done.2, f32[4,384]{1,0:T(4,128)S(1)} %get-tuple-element.220, pred[384,1536]{1,0:T(8,128)(4,1)S(1)} %copy-done.8), kind=kLoop, calls=%fused_computation.35 | loop fusion | flops 9435648 | bytes 10039296 | tf_op jit(solution)/shard_map/while/body/eval_jaxpr/reduce_sum | solution.py:49
  322.6 37.2 %collective-permute-done.5 = bf16[6144,4,128]{0,2,1:T(8,128)(2,1)} collective-permute-done((bf16[6144,4,128]{0,2,1:T(8,128)(2,1)}, bf16[6144,4,128]{0,2,1:T(8,128)(2,1)}, u32[]{:S(2)}, u32[]{:S(2)}) %collective-permute-start.5) | collective-permute-done | bytes 6291488 | tf_op jit(solution)/shard_map/ppermute | solution.py:22
  359.8 15.5 %maximum_select_fusion.1 = bf16[12288,4,128]{0,2,1:T(8,128)(2,1)} fusion(bf16[6144,4,128]{0,2,1:T(8,128)(2,1)} %maximum_select_fusion.3, bf16[6144,4,128]{0,2,1:T(8,128)(2,1)} %collective-permute-done.5, pred[]{:T(512)S(6)} %eq.66), kind=kLoop, calls=%fused_computation.25 | loop fusion | flops 56623104 | bytes 25165824 | tf_op jit(solution)/shard_map/jit(_where)/select_n | solution.py:94
  375.3 16.6 %copy.72 = bf16[12288,4,128]{2,0,1:T(8,128)(2,1)} copy(bf16[12288,4,128]{0,2,1:T(8,128)(2,1)} %maximum_select_fusion.1) | data formatting | bytes 25165824 | tf_op jit(solution)/shard_map/jit(_where)/select_n | solution.py:94
  391.9 101.8 %collective-permute-done.4 = bf16[6144,4,128]{0,2,1:T(8,128)(2,1)} collective-permute-done((bf16[6144,4,128]{0,2,1:T(8,128)(2,1)}, bf16[6144,4,128]{0,2,1:T(8,128)(2,1)}, u32[]{:S(2)}, u32[]{:S(2)}) %collective-permute-start.4) | collective-permute-done | bytes 6291488 | tf_op jit(solution)/shard_map/ppermute | solution.py:22
  493.6 15.6 %maximum_select_fusion = bf16[12288,4,128]{0,2,1:T(8,128)(2,1)} fusion(bf16[6144,4,128]{0,2,1:T(8,128)(2,1)} %maximum_select_fusion.2, bf16[6144,4,128]{0,2,1:T(8,128)(2,1)} %collective-permute-done.4, pred[]{:T(512)S(6)} %eq.66), kind=kLoop, calls=%fused_computation.24 | loop fusion | flops 56623104 | bytes 25165824 | tf_op jit(solution)/shard_map/jit(_where)/select_n | solution.py:94
  509.2 16.6 %copy.70 = bf16[12288,4,128]{2,0,1:T(8,128)(2,1)} copy(bf16[12288,4,128]{0,2,1:T(8,128)(2,1)} %maximum_select_fusion) | data formatting | bytes 25165824 | tf_op jit(solution)/shard_map/jit(_where)/select_n | solution.py:94
  525.8 38.3 %fusion.20 = (bf16[1536,4,128]{2,0,1:T(8,128)(2,1)S(1)}, bf16[1536,4,128]{2,0,1:T(8,128)(2,1)S(1)}) fusion(bf16[12288,4,128]{2,0,1:T(8,128)(2,1)} %copy.72, pred[8,4]{0,1:T(4,128)(4,1)S(1)} %iota_compare_fusion.4, bf16[12288,4,128]{2,0,1:T(8,128)(2,1)} %copy.70), kind=kLoop, calls=%fused_computation.27 | loop fusion | flops 23592960 | bytes 28311584 | tf_op jit(solution)/shard_map/reduce_sum | solution.py:28
  564.1 1.2 fusion.31
  565.3 1.3 fusion.32
  566.6 1.5 fusion.57
  570.5 1.1 broadcast_in_dim.421
  571.6 9.3 %fusion.43 = bf16[1536,4,128]{2,0,1:T(8,128)(2,1)S(1)} fusion(f32[1536,4,128]{2,0,1:T(8,128)S(1)} %bitcast.136, f32[1536,4,128]{2,0,1:T(8,128)S(1)} %bitcast.134, f32[3,512,4,128]{3,1,0,2:T(8,128)S(1)} %copy-done.10, f32[1536,4]{0,1:T(4,128)S(1)} %get-tuple-element.202, f32[1536,4]{0,1:T(4,128)S(1)} %get-tuple-element.208, f32[192,4,128]{2,0,1:T(8,128)S(1)} %fusion.57, ...), kind=kLoop, calls=%fused_computation.64 | loop fusion | flops 11010048 | bytes 11593728 | tf_op jit(solution)/shard_map/convert_element_type | solution.py:139
  582.3 24.1 %all_to_all.5 = bf16[4,384,512]{1,2,0:T(8,128)(2,1)S(1)} all-to-all(bf16[4,384,512]{1,2,0:T(8,128)(2,1)S(1)} %pad_maximum_fusion), channel_id=1, replica_groups=mesh['ctx'=32,'head'=4] {'head'}, dimensions={0} | all-to-all | bytes 3145728 | tf_op jit(solution)/shard_map/all_to_all | solution.py:15
  606.4 8.1 %convolution_convert_fusion = bf16[384,2048]{1,0:T(8,128)(2,1)} fusion(bf16[384,2048]{0,1:T(8,128)(2,1)S(1)} %bitcast.139, bf16[2048,2048]{1,0:T(8,128)(2,1)} %param.11), kind=kOutput, calls=%fused_computation.65 | convolution fusion | flops 3222011904 | bytes 11534336 | tf_op jit(solution)/shard_map/dot_general | solution.py:143
  (97 shorter events, 15.3 us)
Async XLA Ops:
  0.0 20.9 %copy-start = (s32[3,16]{1,0:T(4,128)S(1)}, s32[3,16]{1,0:T(4,128)}, u32[]{:S(2)}) copy-start(s32[3,16]{1,0:T(4,128)} %param.10) | copy-start | bytes 580
  2.6 77.5 %collective-permute-start.1 = (bf16[1536,4,128]{0,2,1:T(8,128)(2,1)}, bf16[1536,4,128]{0,2,1:T(8,128)(2,1)}, u32[]{:S(2)}, u32[]{:S(2)}) collective-permute-start(bf16[1536,4,128]{0,2,1:T(8,128)(2,1)} %bitcast.1), channel_id=1, source_target_pairs={{0,4},{4,0},{8,12},{12,8},{16,20},{20,16},{24,28},{28,24},{32,36},... | collective-permute-start | bytes 4718600 | tf_op jit(solution)/shard_map/ppermute | solution.py:22
  5.2 87.4 %collective-permute-start = (bf16[1536,4,128]{0,2,1:T(8,128)(2,1)}, bf16[1536,4,128]{0,2,1:T(8,128)(2,1)}, u32[]{:S(2)}, u32[]{:S(2)}) collective-permute-start(bf16[1536,4,128]{0,2,1:T(8,128)(2,1)} %bitcast), channel_id=1, source_target_pairs={{0,4},{4,0},{8,12},{12,8},{16,20},{20,16},{24,28},{28,24},{32,36},... | collective-permute-start | bytes 4718600 | tf_op jit(solution)/shard_map/ppermute | solution.py:22
  21.2 65.3 %copy-start.17 = (pred[4,4]{0,1:T(4,128)(4,1)}, pred[4,4]{0,1:T(4,128)(4,1)S(1)}, u32[]{:S(2)}) copy-start(pred[4,4]{0,1:T(4,128)(4,1)S(1)} %iota_compare_fusion.5) | copy-start | bytes 52
  21.3 0.6 copy-start.19
  66.6 13.4 %copy-start.16 = (f32[3,512,4]{1,2,0:T(4,128)}, f32[3,512,4]{1,2,0:T(4,128)S(1)}, u32[]{:S(2)}) copy-start(f32[3,512,4]{1,2,0:T(4,128)S(1)} %get-tuple-element.116) | copy-start | bytes 73732
  66.7 9.8 %copy-start.4 = (bf16[1536,512]{1,0:T(8,128)(2,1)S(1)}, bf16[1536,512]{1,0:T(8,128)(2,1)}, u32[]{:S(2)}) copy-start(bf16[1536,512]{1,0:T(8,128)(2,1)} %param.7) | copy-start | bytes 4718596
  76.4 10.6 %copy-start.20 = (pred[2,4]{0,1:T(4,128)(4,1)S(1)}, pred[2,4]{0,1:T(4,128)(4,1)}, u32[]{:S(2)}) copy-start(pred[2,4]{0,1:T(4,128)(4,1)} %copy-done.19) | copy-start | bytes 28
  83.8 71.2 %collective-permute-start.3 = (bf16[3072,4,128]{0,2,1:T(8,128)(2,1)S(1)}, bf16[3072,4,128]{0,2,1:T(8,128)(2,1)}, u32[]{:S(2)}, u32[]{:S(2)}) collective-permute-start(bf16[3072,4,128]{0,2,1:T(8,128)(2,1)S(1)} %maximum_select_fusion.5), channel_id=1, source_target_pairs={{0,8},{4,12},{8,0},{12,4},{16,24},{20,28},{24,16},{28,20},{32,40},... | collective-permute-start | bytes 9437192 | tf_op jit(solution)/shard_map/ppermute | solution.py:22
  102.2 120.1 %collective-permute-start.2 = (bf16[3072,4,128]{0,2,1:T(8,128)(2,1)}, bf16[3072,4,128]{0,2,1:T(8,128)(2,1)}, u32[]{:S(2)}, u32[]{:S(2)}) collective-permute-start(bf16[3072,4,128]{0,2,1:T(8,128)(2,1)} %maximum_select_fusion.4), channel_id=1, source_target_pairs={{0,8},{4,12},{8,0},{12,4},{16,24},{20,28},{24,16},{28,20},{32,40},... | collective-permute-start | bytes 9437192 | tf_op jit(solution)/shard_map/ppermute | solution.py:22
  102.6 42.2 %copy-start.5 = (pred[768,1536]{1,0:T(8,128)(4,1)S(1)}, pred[768,1536]{1,0:T(8,128)(4,1)}, u32[]{:S(2)}) copy-start(pred[768,1536]{1,0:T(8,128)(4,1)} %iota_compare_fusion.1) | copy-start | bytes 3538948
  102.6 42.2 %copy-start.9 = (bf16[768,4,128]{2,1,0:T(4,128)(2,1)S(1)}, bf16[768,4,128]{2,1,0:T(4,128)(2,1)}, u32[]{:S(2)}) copy-start(bf16[768,4,128]{2,1,0:T(4,128)(2,1)} %select_reduce_fusion.3) | copy-start | bytes 2359300
  162.0 197.7 %collective-permute-start.5 = (bf16[6144,4,128]{0,2,1:T(8,128)(2,1)}, bf16[6144,4,128]{0,2,1:T(8,128)(2,1)}, u32[]{:S(2)}, u32[]{:S(2)}) collective-permute-start(bf16[6144,4,128]{0,2,1:T(8,128)(2,1)} %maximum_select_fusion.3), channel_id=1, source_target_pairs={{0,16},{4,20},{8,24},{12,28},{16,0},{20,4},{24,8},{28,12},{32,48},... | collective-permute-start | bytes 18874376 | tf_op jit(solution)/shard_map/ppermute | solution.py:22
  175.8 46.6 %copy-start.3 = (bf16[3072,4,128]{0,2,1:T(8,128)(2,1)S(1)}, bf16[3072,4,128]{0,2,1:T(8,128)(2,1)}, u32[]{:S(2)}) copy-start(bf16[3072,4,128]{0,2,1:T(8,128)(2,1)} %maximum_select_fusion.4) | copy-start | bytes 9437188
  180.0 52.8 %copy-start.6 = (pred[768,1536]{1,0:T(8,128)(4,1)S(1)}, pred[768,1536]{1,0:T(8,128)(4,1)}, u32[]{:S(2)}) copy-start(pred[768,1536]{1,0:T(8,128)(4,1)} %iota_compare_fusion.1) | copy-start | bytes 3538948
  229.5 13.7 %copy-start.12 = (f32[768,4]{1,0:T(8,128)S(1)}, f32[768,4]{1,0:T(8,128)}, u32[]{:S(2)}) copy-start(f32[768,4]{1,0:T(8,128)} %copy.59) | copy-start | bytes 36868
  229.5 264.1 %collective-permute-start.4 = (bf16[6144,4,128]{0,2,1:T(8,128)(2,1)}, bf16[6144,4,128]{0,2,1:T(8,128)(2,1)}, u32[]{:S(2)}, u32[]{:S(2)}) collective-permute-start(bf16[6144,4,128]{0,2,1:T(8,128)(2,1)} %maximum_select_fusion.2), channel_id=1, source_target_pairs={{0,16},{4,20},{8,24},{12,28},{16,0},{20,4},{24,8},{28,12},{32,48},... | collective-permute-start | bytes 18874376 | tf_op jit(solution)/shard_map/ppermute | solution.py:22
  252.3 8.7 %copy-start.18 = (pred[4,4]{0,1:T(4,128)(4,1)S(1)}, pred[4,4]{0,1:T(4,128)(4,1)}, u32[]{:S(2)}) copy-start(pred[4,4]{0,1:T(4,128)(4,1)} %copy-done.17) | copy-start | bytes 52
  261.0 42.6 %copy-start.8 = (pred[384,1536]{1,0:T(8,128)(4,1)S(1)}, pred[384,1536]{1,0:T(8,128)(4,1)}, u32[]{:S(2)}) copy-start(pred[384,1536]{1,0:T(8,128)(4,1)} %iota_compare_fusion.2) | copy-start | bytes 1769476
  261.0 42.6 %copy-start.11 = (bf16[384,4,128]{2,1,0:T(4,128)(2,1)S(1)}, bf16[384,4,128]{2,1,0:T(4,128)(2,1)}, u32[]{:S(2)}) copy-start(bf16[384,4,128]{2,1,0:T(4,128)(2,1)} %select_reduce_fusion.2) | copy-start | bytes 1179652
  305.7 3.6 copy-start.2
  525.8 38.3 %copy-start.13 = (bf16[192,4,128]{2,1,0:T(4,128)(2,1)S(1)}, bf16[192,4,128]{2,1,0:T(4,128)(2,1)}, u32[]{:S(2)}) copy-start(bf16[192,4,128]{2,1,0:T(4,128)(2,1)} %fusion.50) | copy-start | bytes 589828
  568.1 2.4 copy-start.7
  568.7 2.9 copy-start.14
  568.7 2.9 copy-start.15
  568.9 2.7 copy-start.10
  606.4 8.1 %copy-start.1 = (s32[3,16]{1,0:T(4,128)S(1)}, s32[3,16]{1,0:T(4,128)}, u32[]{:S(2)}) copy-start(s32[3,16]{1,0:T(4,128)} %param.10) | copy-start | bytes 580
